TPU v7x, 32 devices: a whole 2x2x4 slice. The times are simulated.
32 devices in a mesh: row: 8 (over z, y), col: 4 (over x, core).
Axes of the slice: x: 2, y: 2, z: 4, core: 2. Of those that a mesh axis runs over, the one named last changes fastest.
Arguments:
- rhs_grid: float32 [65536, 512], P(('row', 'col')), may hold values from -6 to 6
- leaf_order: int32 [128, 512], P(('row', 'col')), may hold values from 0 to 511, each once within a row
- source_basis: float32 [128, 512, 192], P(('row', 'col')), may hold values from -0.25 to 0.25
- transfer: float32 [7, 128, 192, 384], P(None, ('row', 'col')), may hold values from -0.3125 to 0.3125
- target_basis: float32 [128, 512, 192], P(('row', 'col')), may hold values from -0.4375 to 0.4375
Outputs:
- result: float32 [65536, 512], P(('row', 'col'))
Inputs may be any that keep to these rules, and one draw needn't show every extreme that they name: Each row of leaf_order names every one of 0 to 511 once.
All inputs are finite; a program needn't handle non-finite values.
Results may differ from a plain program's by a relative error of at most 0.00013.
Values sent between devices are 32-bit elements; how exact they have to be, the bound alone decides.
A program may use at most 128 MiB of HBM per device.

v0:
```python
import functools

import jax
import jax.numpy as jnp
from jax import lax
from jax.experimental import pallas as pl
from jax.experimental.pallas import tpu as pltpu
from jax.sharding import PartitionSpec as P

F32 = jnp.float32
BF16 = jnp.bfloat16
WIDTH = 128
MIDDLE = 2
FAR = 3
PLACE_AT = 6


def split(value):
    high = value.astype(BF16)
    return high, (value - high.astype(F32)).astype(BF16)


def dot(a, b):
    return jnp.dot(a, b, preferred_element_type=F32)


def dot3(a_parts, b_parts):
    (a_high, a_low), (b_high, b_low) = a_parts, b_parts
    width = b_high.shape[1]
    both = dot(a_high, jnp.concatenate([b_high, b_low], axis=1))
    return both[:, :width] + (both[:, width:] + dot(a_low, b_high))


def partner_id(axis, bit_pos):
    mask = 2**bit_pos
    here = lax.axis_index(axis)
    return {axis: here + mask * (1 - 2 * ((here // mask) % 2))}


def kernel(
    stages, offsets, low_bits,
    rhs, order, source, transfer, target, out, placed,
    rhs_v, source_v, target_v, transfer_v, in_high, in_low, placed_v,
    sent, received, staged, rhs_sem, load_sem, transfer_sem, send_sem, recv_sem, out_sem, placed_sem,
):
    leaf_count, leaf_rows = order.shape
    chunks = rhs_v.shape[0]
    units = leaf_count * chunks

    load_target = pltpu.make_async_copy(target, target_v, load_sem.at[leaf_count])

    def load_source(leaf):
        return pltpu.make_async_copy(source.at[leaf], source_v.at[leaf], load_sem.at[leaf])

    def load_rhs(chunk):
        return pltpu.make_async_copy(
            rhs.at[:, pl.ds(pl.multiple_of(chunk * WIDTH, WIDTH), WIDTH)], rhs_v.at[chunk], rhs_sem.at[chunk]
        )

    def load_transfer(level):
        return pltpu.make_async_copy(transfer.at[level], transfer_v.at[level], transfer_sem.at[level])

    levels = transfer.shape[0]
    for leaf in range(leaf_count):
        load_source(leaf).start()
    load_rhs(0).start()
    for level in range(low_bits + 2):
        load_transfer(level).start()
    load_rhs(1).start()
    for level in range(low_bits + 2, levels):
        load_transfer(level).start()
    for chunk in range(2, chunks):
        load_rhs(chunk).start()
    load_target.start()

    barrier = pltpu.get_barrier_semaphore()
    for stage in stages:
        pl.semaphore_signal(barrier, inc=1, device_id=partner_id(*stage), device_id_type=pl.DeviceIdType.MESH)

    def selection(leaf):
        grid_row = lax.broadcasted_iota(jnp.int32, (leaf_rows, leaf_rows), 0)
        named = jnp.broadcast_to(order[pl.ds(leaf, 1), :], (leaf_rows, leaf_rows))
        return jnp.where(grid_row == named, 1.0, 0.0).astype(BF16)

    def place_in(leaf):
        parts = jnp.concatenate(split(source_v[leaf]), axis=0)
        rows = lax.dot_general(
            parts, selection(leaf), (((1,), (1,)), ((), ())), preferred_element_type=F32
        ).astype(BF16)
        in_high[leaf] = rows[: source_v.shape[1]]
        in_low[leaf] = rows[source_v.shape[1] :]

    def place_out(leaf):
        chosen = selection(leaf)
        for index, part in enumerate(split(target_v[leaf])):
            placed_v[leaf, index] = lax.dot_general(
                chosen, part, (((1,), (1,)), ((), ())), preferred_element_type=F32
            ).astype(BF16)
        write_placed(leaf).start()

    def write_placed(leaf):
        return pltpu.make_async_copy(placed_v.at[leaf], placed.at[leaf], placed_sem.at[leaf])

    def exchange(stage, unit):
        return pltpu.make_async_remote_copy(
            src_ref=sent.at[stage, unit],
            dst_ref=received.at[stage, unit],
            send_sem=send_sem.at[stage, unit],
            recv_sem=recv_sem.at[stage, unit],
            device_id=partner_id(*stages[stage]),
            device_id_type=pl.DeviceIdType.MESH,
        )

    def write_out(unit):
        leaf, chunk = unit % leaf_count, unit // leaf_count
        return pltpu.make_async_copy(
            staged.at[unit],
            out.at[leaf, :, :, pl.ds(pl.multiple_of(chunk * WIDTH, WIDTH), WIDTH)],
            out_sem.at[unit],
        )

    def combine(level, node, own, other):
        return dot3(split(transfer_v[level, node]), split(jnp.concatenate([own, other], axis=0)))

    def enter(chunk):
        load_rhs(chunk).wait()
        current = []
        for leaf in range(leaf_count):
            rows = rhs_v[chunk, pl.ds(leaf * leaf_rows, leaf_rows), :]
            current.append(dot3((in_high[leaf], in_low[leaf]), split(rows)))
        for level in range(low_bits - 1):
            current = [
                combine(level, node, current[node], current[node ^ 2**level]) for node in range(leaf_count)
            ]
        last = low_bits - 1
        for node in range(leaf_count):
            unit = chunk * leaf_count + node
            if low_bits:
                sent[0, unit] = combine(last, node, current[node], current[node ^ 2**last])
            else:
                sent[0, unit] = current[node]
            exchange(0, unit).start()

    def advance(stage, unit):
        node = unit % leaf_count
        exchange(stage, unit).wait_recv()
        value = combine(low_bits + stage, node, sent[stage, unit], received[stage, unit])
        if stage + 1 < len(stages):
            sent[stage + 1, unit] = value
            exchange(stage + 1, unit).start()
        else:
            for index, part in enumerate(split(value)):
                staged[unit, index] = part
            write_out(unit).start()

    for leaf in range(leaf_count):
        load_source(leaf).wait()
        place_in(leaf)
    for level in range(low_bits):
        load_transfer(level).wait()
    pl.semaphore_wait(barrier, len(stages))
    enter(0)

    near = [stage for stage in range(len(stages)) if stages[stage] == ("col", 0)]
    turns = near + [stage for stage in reversed(range(len(stages))) if stage not in near]

    @pl.loop(0, units + offsets[-1])
    def _(tick):
        for stage in turns:
            unit = tick - offsets[stage]

            @pl.when(unit == 0)
            def _():
                load_transfer(low_bits + stage).wait()

            @pl.when((unit >= 0) & (unit < units))
            def _():
                advance(stage, unit)

        @pl.when(tick == PLACE_AT - 1)
        def _():
            load_target.wait()

        @pl.when((tick >= PLACE_AT) & (tick < PLACE_AT + leaf_count))
        def _():
            place_out(tick - PLACE_AT)

        @pl.when((tick % leaf_count == 1) & (tick // leaf_count + 1 < chunks))
        def _():
            enter(tick // leaf_count + 1)

    @pl.loop(0, units)
    def _(unit):
        for stage in range(len(stages)):
            exchange(stage, unit).wait_send()
        write_out(unit).wait()

    @pl.loop(0, leaf_count)
    def _(leaf):
        write_placed(leaf).wait()


def output_kernel(placed, skeleton, out, placed_v, skeleton_v, out_v, placed_sem, skeleton_sem, out_sem):
    leaf_count, _, leaf_rows, _ = placed_v.shape

    def loads(leaf):
        return (
            pltpu.make_async_copy(placed.at[leaf], placed_v.at[leaf], placed_sem.at[leaf]),
            pltpu.make_async_copy(skeleton.at[leaf], skeleton_v.at[leaf], skeleton_sem.at[leaf]),
        )

    def store(leaf):
        return pltpu.make_async_copy(out_v.at[leaf], out.at[pl.ds(leaf * leaf_rows, leaf_rows), :], out_sem.at[leaf])

    for leaf in range(leaf_count):
        for copy in loads(leaf):
            copy.start()
    for leaf in range(leaf_count):
        for copy in loads(leaf):
            copy.wait()
        out_v[leaf] = dot3((placed_v[leaf, 0], placed_v[leaf, 1]), (skeleton_v[leaf, 0], skeleton_v[leaf, 1]))
        store(leaf).start()
    for leaf in range(leaf_count):
        store(leaf).wait()


def on_device(rhs_grid, leaf_order, source_basis, transfer, target_basis):
    leaf_count, leaf_rows = leaf_order.shape
    points, columns = rhs_grid.shape
    rank = source_basis.shape[2]
    levels = transfer.shape[0]
    low_bits = leaf_count.bit_length() - 1
    row_bits = lax.axis_size("row").bit_length() - 1
    col_bits = lax.axis_size("col").bit_length() - 1
    stages = [("row", bit) for bit in range(row_bits)] + [("col", bit) for bit in range(col_bits)]
    count = len(stages)
    offsets = [0]
    for axis, bit in stages[1:]:
        if axis == "col":
            offsets.append(offsets[-1] + 1)
        else:
            offsets.append(offsets[-1] + (FAR if bit == row_bits - 1 else MIDDLE))
    chunks = columns // WIDTH
    units = leaf_count * chunks
    hbm = pl.BlockSpec(memory_space=pl.ANY)
    skeleton, placed = pl.pallas_call(
        functools.partial(kernel, stages, offsets, low_bits),
        out_shape=[
            jax.ShapeDtypeStruct((leaf_count, 2, rank, columns), BF16),
            jax.ShapeDtypeStruct((leaf_count, 2, leaf_rows, rank), BF16),
        ],
        in_specs=[hbm, pl.BlockSpec(memory_space=pltpu.VMEM), hbm, hbm, hbm],
        out_specs=[hbm, hbm],
        scratch_shapes=[
            pltpu.VMEM((chunks, points, WIDTH), F32),
            pltpu.VMEM((leaf_count, rank, leaf_rows), F32),
            pltpu.VMEM((leaf_count, rank, leaf_rows), F32),
            pltpu.VMEM(transfer.shape, F32),
            pltpu.VMEM((leaf_count, rank, leaf_rows), BF16),
            pltpu.VMEM((leaf_count, rank, leaf_rows), BF16),
            pltpu.VMEM((leaf_count, 2, leaf_rows, rank), BF16),
            pltpu.VMEM((count, units, rank, WIDTH), F32),
            pltpu.VMEM((count, units, rank, WIDTH), F32),
            pltpu.VMEM((units, 2, rank, WIDTH), BF16),
            pltpu.SemaphoreType.DMA((chunks,)),
            pltpu.SemaphoreType.DMA((leaf_count + 1,)),
            pltpu.SemaphoreType.DMA((levels,)),
            pltpu.SemaphoreType.DMA((count, units)),
            pltpu.SemaphoreType.DMA((count, units)),
            pltpu.SemaphoreType.DMA((units,)),
            pltpu.SemaphoreType.DMA((leaf_count,)),
        ],
        compiler_params=pltpu.CompilerParams(
            collective_id=0, has_side_effects=True, vmem_limit_bytes=56 * 2**20
        ),
    )(rhs_grid, leaf_order, source_basis.swapaxes(1, 2), transfer, target_basis.swapaxes(1, 2))
    return pl.pallas_call(
        output_kernel,
        out_shape=jax.ShapeDtypeStruct((points, columns), F32),
        in_specs=[hbm, hbm],
        out_specs=hbm,
        scratch_shapes=[
            pltpu.VMEM(placed.shape, BF16),
            pltpu.VMEM(skeleton.shape, BF16),
            pltpu.VMEM((leaf_count, leaf_rows, columns), F32),
            pltpu.SemaphoreType.DMA((leaf_count,)),
            pltpu.SemaphoreType.DMA((leaf_count,)),
            pltpu.SemaphoreType.DMA((leaf_count,)),
        ],
        compiler_params=pltpu.CompilerParams(vmem_limit_bytes=56 * 2**20),
    )(placed, skeleton)


def solution(mesh):
    in_specs = (
        P(("row", "col"), None),
        P(("row", "col"), None),
        P(("row", "col"), None, None),
        P(None, ("row", "col"), None, None),
        P(("row", "col"), None, None),
    )
    out_specs = P(("row", "col"), None)
    return jax.shard_map(
        on_device, mesh=mesh, in_specs=in_specs, out_specs=out_specs, check_vma=False
    )
```

profile of v0, /device:TPU:0, one launch (start us, length us, event | category | flops | bytes accessed | tf_op | source)
XLA Modules:
  0.0 100.8 jit_solution(2544418153323498631)
XLA Ops:
  0.0 96.3 %shard_map.55 = (bf16[4,2,192,512]{3,2,1,0:T(8,128)(2,1)}, bf16[4,2,512,192]{3,2,1,0:T(8,128)(2,1)}) custom-call(f32[2048,512]{1,0:T(8,128)} %rhs.1, s32[4,512]{1,0:T(4,128)} %order.1, f32[4,192,512]{2,1,0:T(8,128)} %bitcast.2, f32[7,4,192,384]{3,2,1,0:T(8,128)} %transfer.1, f32[4,192,512]{2,1,0:T(8,128)} %bitcast.3), custom_call_target="tpu_custom_call" | custom-call | tf_op jit(solution)/shard_map/pallas_call | solution.py:246
  96.3 4.5 %shard_map.56 = f32[2048,512]{1,0:T(8,128)} custom-call(bf16[4,2,512,192]{3,2,1,0:T(8,128)(2,1)} %get-tuple-element.7.placed, bf16[4,2,192,512]{3,2,1,0:T(8,128)(2,1)} %get-tuple-element.8.skeleton), custom_call_target="tpu_custom_call" | custom-call | tf_op jit(solution)/shard_map/pallas_call | solution.py:277
where the time goes:
time: 101 us
  Pallas kernels  101 us (100%)
    pallas_call x1, Pallas kernels, on_device(): pl.pallas_call(functools.partial(kernel, stages, offsets, low_bits), out_...  96.3 us
    pallas_call x1, Pallas kernels, on_device(): pl.pallas_call(output_kernel, out_shape=jax.ShapeDtypeStruct((points, col...  4.48 us

commit v1 on v0

v1 whole, which is shorter than its diff:
```python
import functools

import jax
import jax.numpy as jnp
from jax import lax
from jax.experimental import pallas as pl
from jax.experimental.pallas import tpu as pltpu
from jax.sharding import PartitionSpec as P

F32 = jnp.float32
BF16 = jnp.bfloat16
WIDTH = 128
MIDDLE = 2
FAR = 3
LEAD = 2
SLOTS = 4
VMEM_BYTES = 67043328


def split(value):
    high = value.astype(BF16)
    return high, (value - high.astype(F32)).astype(BF16)


def dot(a, b):
    return jnp.dot(a, b, preferred_element_type=F32)


def dot3(a_high, a_low, b):
    b_high, b_low = split(b)
    width = b.shape[1]
    both = dot(a_high, jnp.concatenate([b_high, b_low], axis=1))
    return both[:, :width] + (both[:, width:] + dot(a_low, b_high))


def partner_id(axis, bit_pos):
    mask = 2**bit_pos
    here = lax.axis_index(axis)
    return {axis: here + mask * (1 - 2 * ((here // mask) % 2))}


def kernel(
    stages, offsets, low_bits,
    rhs, order, source, transfer, target, out,
    order_v, chosen, rhs_v, source_v, target_v, transfer_v, local_t, stage_t, in_v, placed_v,
    sent, received, order_sem, rhs_sem, load_sem, transfer_sem, send_sem, recv_sem,
):
    leaf_count, leaf_rows = order.shape
    chunks = rhs_v.shape[0]
    units = leaf_count * chunks
    levels = transfer.shape[0]
    rank = source_v.shape[1]
    count = len(stages)

    load_order = pltpu.make_async_copy(order, order_v, order_sem)
    load_target = pltpu.make_async_copy(target, target_v, load_sem.at[leaf_count])

    def load_source(leaf):
        return pltpu.make_async_copy(source.at[leaf], source_v.at[leaf], load_sem.at[leaf])

    def load_rhs(chunk):
        return pltpu.make_async_copy(
            rhs.at[:, pl.ds(pl.multiple_of(chunk * WIDTH, WIDTH), WIDTH)], rhs_v.at[chunk], rhs_sem.at[chunk]
        )

    def load_transfer(level):
        return pltpu.make_async_copy(transfer.at[level], transfer_v.at[level % SLOTS], transfer_sem.at[level])

    def select(leaf):
        grid_row = lax.broadcasted_iota(jnp.int32, (leaf_rows, leaf_rows), 0)
        named = jnp.broadcast_to(order_v[pl.ds(leaf, 1), :], (leaf_rows, leaf_rows))
        chosen[leaf] = jnp.where(grid_row == named, 1.0, 0.0).astype(BF16)

    def place_in(leaf):
        parts = jnp.concatenate(split(source_v[leaf]), axis=0)
        in_v[leaf] = lax.dot_general(
            parts, chosen[leaf], (((1,), (1,)), ((), ())), preferred_element_type=F32
        ).astype(BF16)

    def place_out(leaf):
        for index, part in enumerate(split(target_v[leaf])):
            placed_v[leaf, index] = lax.dot_general(
                chosen[leaf], part, (((1,), (1,)), ((), ())), preferred_element_type=F32
            ).astype(BF16)

    def prepare_local(level):
        load_transfer(level).wait()
        for node in range(leaf_count):
            for index, part in enumerate(split(transfer_v[level % SLOTS, node])):
                local_t[level, node, index] = part

    def prepare(stage):
        level = low_bits + stage
        load_transfer(level).wait()

        @pl.loop(0, leaf_count)
        def _(node):
            for index, part in enumerate(split(transfer_v[level % SLOTS, node])):
                stage_t[stage, node, index, 0] = part[:, :rank]
                stage_t[stage, node, index, 1] = part[:, rank:]

        if level + SLOTS < levels:
            load_transfer(level + SLOTS).start()

    def exchange(stage, unit):
        return pltpu.make_async_remote_copy(
            src_ref=sent.at[stage, unit],
            dst_ref=received.at[stage, unit],
            send_sem=send_sem.at[stage, unit],
            recv_sem=recv_sem.at[stage, unit],
            device_id=partner_id(*stages[stage]),
            device_id_type=pl.DeviceIdType.MESH,
        )

    def half(stage, node, side, value):
        return dot3(stage_t[stage, node, 0, side], stage_t[stage, node, 1, side], value)

    def combine(level, node, own, other):
        return dot3(local_t[level, node, 0], local_t[level, node, 1], jnp.concatenate([own, other], axis=0))

    def enter(chunk, first=False):
        load_rhs(chunk).wait()
        current = {}
        for leaf in range(leaf_count):
            rows = rhs_v[chunk, pl.ds(leaf * leaf_rows, leaf_rows), :]
            current[0, leaf] = dot3(in_v[leaf, :rank], in_v[leaf, rank:], rows)

        def value_of(level, node):
            if (level, node) not in current:
                bit = level - 1
                if first and all((level, other) not in current for other in range(leaf_count)):
                    prepare_local(bit)
                current[level, node] = combine(bit, node, value_of(bit, node), value_of(bit, node ^ 2**bit))
            return current[level, node]

        for node in range(leaf_count):
            unit = chunk * leaf_count + node
            sent[0, unit] = value_of(low_bits, node)
            if first and node == 0:
                pl.semaphore_wait(barrier, count)
            if first and node < LEAD:
                exchange(0, unit).start()

    def advance(stage, unit):
        node = unit % leaf_count
        own = half(stage, node, 0, sent[stage, unit])
        exchange(stage, unit).wait_recv()
        value = own + half(stage, node, 1, received[stage, unit])
        if stage + 1 < count:
            sent[stage + 1, unit] = value
            exchange(stage + 1, unit).start()
        else:
            chunk = unit // leaf_count
            rows = pl.ds(pl.multiple_of(node * leaf_rows, leaf_rows), leaf_rows)
            cols = pl.ds(pl.multiple_of(chunk * WIDTH, WIDTH), WIDTH)
            out[rows, cols] = dot3(placed_v[node, 0], placed_v[node, 1], value)

    load_order.start()
    for leaf in range(leaf_count):
        load_source(leaf).start()
    load_rhs(0).start()
    barrier = pltpu.get_barrier_semaphore()
    for stage in stages:
        pl.semaphore_signal(barrier, inc=1, device_id=partner_id(*stage), device_id_type=pl.DeviceIdType.MESH)
    load_order.wait()
    for level in range(low_bits):
        load_transfer(level).start()
    for leaf in range(leaf_count):
        select(leaf)
    for leaf in range(leaf_count):
        load_source(leaf).wait()
        place_in(leaf)
    for level in range(low_bits, min(SLOTS, levels)):
        load_transfer(level).start()
    load_rhs(1).start()
    enter(0, first=True)
    for level in range(SLOTS, min(SLOTS + low_bits, levels)):
        load_transfer(level).start()
    load_target.start()
    for chunk in range(2, chunks):
        load_rhs(chunk).start()
    prepare(0)
    prepare(1)
    enter(1)

    near = [stage for stage in range(count) if stages[stage] == ("col", 0)]
    turns = near + [stage for stage in reversed(range(count)) if stage not in near]

    @pl.loop(0, units + offsets[-1])
    def _(tick):
        @pl.when(tick + LEAD < units)
        def _():
            exchange(0, tick + LEAD).start()

        for stage in turns:
            unit = tick - offsets[stage]

            @pl.when((unit >= 0) & (unit < units))
            def _():
                advance(stage, unit)

        for stage in range(2, count):

            @pl.when(tick == stage - 2)
            def _():
                prepare(stage)

        @pl.when((tick >= offsets[-1] - leaf_count) & (tick < offsets[-1]))
        def _():
            leaf = tick - (offsets[-1] - leaf_count)

            @pl.when(leaf == 0)
            def _():
                load_target.wait()

            place_out(leaf)

        @pl.when((tick % leaf_count == 1) & (tick // leaf_count + 2 < chunks))
        def _():
            enter(tick // leaf_count + 2)

        done = tick - offsets[-1] - 1

        @pl.when(done >= 0)
        def _():
            for stage in range(count):
                exchange(stage, done).wait_send()

    for stage in range(count):
        exchange(stage, units - 1).wait_send()


def output_kernel(result, out, sem):
    pieces = sem.shape[0]
    rows = out.shape[0] // pieces

    def store(piece):
        at = pl.ds(piece * rows, rows)
        return pltpu.make_async_copy(result.at[at, :], out.at[at, :], sem.at[piece])

    for piece in range(pieces):
        store(piece).start()
    for piece in range(pieces):
        store(piece).wait()


def on_device(rhs_grid, leaf_order, source_basis, transfer, target_basis):
    leaf_count, leaf_rows = leaf_order.shape
    points, columns = rhs_grid.shape
    rank = source_basis.shape[2]
    levels = transfer.shape[0]
    low_bits = leaf_count.bit_length() - 1
    row_bits = lax.axis_size("row").bit_length() - 1
    col_bits = lax.axis_size("col").bit_length() - 1
    stages = [("row", bit) for bit in range(row_bits)] + [("col", bit) for bit in range(col_bits)]
    count = len(stages)
    offsets = [0]
    for axis, bit in stages[1:]:
        if axis == "col":
            offsets.append(offsets[-1] + 1)
        else:
            offsets.append(offsets[-1] + (FAR if bit == row_bits - 1 else MIDDLE))
    chunks = columns // WIDTH
    units = leaf_count * chunks
    hbm = pl.BlockSpec(memory_space=pl.ANY)
    vmem = pl.BlockSpec(memory_space=pltpu.VMEM)
    result = pl.pallas_call(
        functools.partial(kernel, stages, offsets, low_bits),
        out_shape=pltpu.VMEM((points, columns), F32),
        in_specs=[hbm, hbm, hbm, hbm, hbm],
        out_specs=vmem,
        scratch_shapes=[
            pltpu.VMEM((leaf_count, leaf_rows), jnp.int32),
            pltpu.VMEM((leaf_count, leaf_rows, leaf_rows), BF16),
            pltpu.VMEM((chunks, points, WIDTH), F32),
            pltpu.VMEM((leaf_count, rank, leaf_rows), F32),
            pltpu.VMEM((leaf_count, rank, leaf_rows), F32),
            pltpu.VMEM((SLOTS,) + transfer.shape[1:], F32),
            pltpu.VMEM((low_bits, leaf_count, 2, rank, 2 * rank), BF16),
            pltpu.VMEM((count, leaf_count, 2, 2, rank, rank), BF16),
            pltpu.VMEM((leaf_count, 2 * rank, leaf_rows), BF16),
            pltpu.VMEM((leaf_count, 2, leaf_rows, rank), BF16),
            pltpu.VMEM((count, units, rank, WIDTH), F32),
            pltpu.VMEM((count, units, rank, WIDTH), F32),
            pltpu.SemaphoreType.DMA,
            pltpu.SemaphoreType.DMA((chunks,)),
            pltpu.SemaphoreType.DMA((leaf_count + 1,)),
            pltpu.SemaphoreType.DMA((levels,)),
            pltpu.SemaphoreType.DMA((count, units)),
            pltpu.SemaphoreType.DMA((count, units)),
        ],
        compiler_params=pltpu.CompilerParams(
            collective_id=0, has_side_effects=True, vmem_limit_bytes=VMEM_BYTES - 4 * points * columns - 2**18
        ),
    )(rhs_grid, leaf_order, source_basis.swapaxes(1, 2), transfer, target_basis.swapaxes(1, 2))
    return pl.pallas_call(
        output_kernel,
        out_shape=jax.ShapeDtypeStruct((points, columns), F32),
        in_specs=[vmem],
        out_specs=hbm,
        scratch_shapes=[pltpu.SemaphoreType.DMA((2 * leaf_count,))],
        compiler_params=pltpu.CompilerParams(vmem_limit_bytes=2**20),
    )(result)


def solution(mesh):
    in_specs = (
        P(("row", "col"), None),
        P(("row", "col"), None),
        P(("row", "col"), None, None),
        P(None, ("row", "col"), None, None),
        P(("row", "col"), None, None),
    )
    out_specs = P(("row", "col"), None)
    return jax.shard_map(
        on_device, mesh=mesh, in_specs=in_specs, out_specs=out_specs, check_vma=False
    )
```

time: 101 us -> 96.9 us (0.959)
  Pallas kernels: 101 us -> 96.7 us
    pallas_call x1, Pallas kernels: 4.48 us -> 2.07 us  [on_device(): pl.pallas_call(output_kernel, out_shape=jax.ShapeDtypeStruct((points, col...]
    pallas_call x1, Pallas kernels: 96.3 us -> 94.7 us  [on_device(): pl.pallas_call(functools.partial(kernel, stages, offsets, low_bits), out_...]
where the time goes in v1:
time: 96.9 us; the launch traced here: 96.7 us
  Pallas kernels  96.7 us (100%)
    pallas_call x1, Pallas kernels, on_device(): pl.pallas_call(functools.partial(kernel, stages, offsets, low_bits), out_...  94.7 us
    pallas_call x1, Pallas kernels, on_device(): pl.pallas_call(output_kernel, out_shape=jax.ShapeDtypeStruct((points, col...  2.07 us

profile of v1, /device:TPU:0, one launch (start us, length us, event | category | flops | bytes accessed | tf_op | source)
XLA Modules:
  0.0 96.7 jit_solution(9272237426160213089)
XLA Ops:
  0.0 94.7 %shard_map.55.result = f32[2048,512]{1,0:T(8,128)S(1)} custom-call(f32[2048,512]{1,0:T(8,128)} %rhs.1, s32[4,512]{1,0:T(4,128)} %order.1, f32[4,192,512]{2,1,0:T(8,128)} %bitcast.2, f32[7,4,192,384]{3,2,1,0:T(8,128)} %transfer.1, f32[4,192,512]{2,1,0:T(8,128)} %bitcast.3), custom_call_target="tpu_custom_call" | custom-call | tf_op jit(solution)/shard_map/pallas_call | solution.py:267
  94.7 2.1 %shard_map.56 = f32[2048,512]{1,0:T(8,128)} custom-call(f32[2048,512]{1,0:T(8,128)S(1)} %shard_map.55.result), custom_call_target="tpu_custom_call" | custom-call | tf_op jit(solution)/shard_map/pallas_call | solution.py:296

commit v2 on v1

--- a/solution.py
+++ b/solution.py
@@ -12,8 +12,9 @@
 WIDTH = 128
 MIDDLE = 2
 FAR = 3
-LEAD = 2
 SLOTS = 4
+LEAD = 1
+FLIGHT = 8
 VMEM_BYTES = 67043328
 
 
@@ -43,7 +44,7 @@
     stages, offsets, low_bits,
     rhs, order, source, transfer, target, out,
     order_v, chosen, rhs_v, source_v, target_v, transfer_v, local_t, stage_t, in_v, placed_v,
-    sent, received, order_sem, rhs_sem, load_sem, transfer_sem, send_sem, recv_sem,
+    sent, received, load_sem, rhs_sem, transfer_sem, send_sem, recv_sem,
 ):
     leaf_count, leaf_rows = order.shape
     chunks = rhs_v.shape[0]
@@ -52,11 +53,9 @@
     rank = source_v.shape[1]
     count = len(stages)
 
-    load_order = pltpu.make_async_copy(order, order_v, order_sem)
-    load_target = pltpu.make_async_copy(target, target_v, load_sem.at[leaf_count])
-
-    def load_source(leaf):
-        return pltpu.make_async_copy(source.at[leaf], source_v.at[leaf], load_sem.at[leaf])
+    load_order = pltpu.make_async_copy(order, order_v, load_sem.at[0])
+    load_source = pltpu.make_async_copy(source, source_v, load_sem.at[1])
+    load_target = pltpu.make_async_copy(target, target_v, load_sem.at[2])
 
     def load_rhs(chunk):
         return pltpu.make_async_copy(
@@ -64,7 +63,12 @@
         )
 
     def load_transfer(level):
-        return pltpu.make_async_copy(transfer.at[level], transfer_v.at[level % SLOTS], transfer_sem.at[level])
+        return pltpu.make_async_copy(
+            transfer.at[level], transfer_v.at[level % SLOTS], transfer_sem.at[max(level - low_bits + 1, 0)]
+        )
+
+    low_slots = transfer_v.at[pl.ds(0, low_bits)]
+    low_transfer = pltpu.make_async_copy(low_slots, low_slots, transfer_sem.at[0])
 
     def select(leaf):
         grid_row = lax.broadcasted_iota(jnp.int32, (leaf_rows, leaf_rows), 0)
@@ -84,7 +88,6 @@
             ).astype(BF16)
 
     def prepare_local(level):
-        load_transfer(level).wait()
         for node in range(leaf_count):
             for index, part in enumerate(split(transfer_v[level % SLOTS, node])):
                 local_t[level, node, index] = part
@@ -106,8 +109,8 @@
         return pltpu.make_async_remote_copy(
             src_ref=sent.at[stage, unit],
             dst_ref=received.at[stage, unit],
-            send_sem=send_sem.at[stage, unit],
-            recv_sem=recv_sem.at[stage, unit],
+            send_sem=send_sem,
+            recv_sem=recv_sem.at[stage, unit % FLIGHT],
             device_id=partner_id(*stages[stage]),
             device_id_type=pl.DeviceIdType.MESH,
         )
@@ -145,6 +148,12 @@
         node = unit % leaf_count
         own = half(stage, node, 0, sent[stage, unit])
         exchange(stage, unit).wait_recv()
+        if stage == 0:
+
+            @pl.when(unit + LEAD < units)
+            def _():
+                exchange(0, unit + LEAD).start()
+
         value = own + half(stage, node, 1, received[stage, unit])
         if stage + 1 < count:
             sent[stage + 1, unit] = value
@@ -156,8 +165,7 @@
             out[rows, cols] = dot3(placed_v[node, 0], placed_v[node, 1], value)
 
     load_order.start()
-    for leaf in range(leaf_count):
-        load_source(leaf).start()
+    load_source.start()
     load_rhs(0).start()
     barrier = pltpu.get_barrier_semaphore()
     for stage in stages:
@@ -167,12 +175,14 @@
         load_transfer(level).start()
     for leaf in range(leaf_count):
         select(leaf)
+    load_source.wait()
     for leaf in range(leaf_count):
-        load_source(leaf).wait()
         place_in(leaf)
     for level in range(low_bits, min(SLOTS, levels)):
         load_transfer(level).start()
     load_rhs(1).start()
+    if low_bits:
+        low_transfer.wait()
     enter(0, first=True)
     for level in range(SLOTS, min(SLOTS + low_bits, levels)):
         load_transfer(level).start()
@@ -181,17 +191,12 @@
         load_rhs(chunk).start()
     prepare(0)
     prepare(1)
-    enter(1)
 
     near = [stage for stage in range(count) if stages[stage] == ("col", 0)]
     turns = near + [stage for stage in reversed(range(count)) if stage not in near]
 
     @pl.loop(0, units + offsets[-1])
     def _(tick):
-        @pl.when(tick + LEAD < units)
-        def _():
-            exchange(0, tick + LEAD).start()
-
         for stage in turns:
             unit = tick - offsets[stage]
 
@@ -215,19 +220,11 @@
 
             place_out(leaf)
 
-        @pl.when((tick % leaf_count == 1) & (tick // leaf_count + 2 < chunks))
+        @pl.when((tick % leaf_count == 1) & (tick // leaf_count + 1 < chunks))
         def _():
-            enter(tick // leaf_count + 2)
-
-        done = tick - offsets[-1] - 1
-
-        @pl.when(done >= 0)
-        def _():
-            for stage in range(count):
-                exchange(stage, done).wait_send()
-
-    for stage in range(count):
-        exchange(stage, units - 1).wait_send()
+            enter(tick // leaf_count + 1)
+
+    pltpu.make_async_copy(sent, sent, send_sem).wait()
 
 
 def output_kernel(result, out, sem):
@@ -282,12 +279,11 @@
             pltpu.VMEM((leaf_count, 2, leaf_rows, rank), BF16),
             pltpu.VMEM((count, units, rank, WIDTH), F32),
             pltpu.VMEM((count, units, rank, WIDTH), F32),
+            pltpu.SemaphoreType.DMA((3,)),
+            pltpu.SemaphoreType.DMA((chunks,)),
+            pltpu.SemaphoreType.DMA((count + 1,)),
             pltpu.SemaphoreType.DMA,
-            pltpu.SemaphoreType.DMA((chunks,)),
-            pltpu.SemaphoreType.DMA((leaf_count + 1,)),
-            pltpu.SemaphoreType.DMA((levels,)),
-            pltpu.SemaphoreType.DMA((count, units)),
-            pltpu.SemaphoreType.DMA((count, units)),
+            pltpu.SemaphoreType.DMA((count, FLIGHT)),
         ],
         compiler_params=pltpu.CompilerParams(
             collective_id=0, has_side_effects=True, vmem_limit_bytes=VMEM_BYTES - 4 * points * columns - 2**18

time: 96.9 us -> 95.2 us (0.982)
  Pallas kernels: 96.7 us -> 94.9 us
    pallas_call x1, Pallas kernels: 94.7 us -> 92.9 us  [on_device(): pl.pallas_call(functools.partial(kernel, stages, offsets, low_bits), out_...]
where the time goes in v2:
time: 95.2 us; the launch traced here: 94.9 us
  Pallas kernels  94.9 us (100%)
    pallas_call x1, Pallas kernels, on_device(): pl.pallas_call(functools.partial(kernel, stages, offsets, low_bits), out_...  92.9 us
    pallas_call x1, Pallas kernels, on_device(): pl.pallas_call(output_kernel, out_shape=jax.ShapeDtypeStruct((points, col...  2.07 us

profile of v2, /device:TPU:0, one launch (start us, length us, event | category | flops | bytes accessed | tf_op | source)
XLA Modules:
  0.0 94.9 jit_solution(15501333125274846015)
XLA Ops:
  0.0 92.9 %shard_map.55.result = f32[2048,512]{1,0:T(8,128)S(1)} custom-call(f32[2048,512]{1,0:T(8,128)} %rhs.1, s32[4,512]{1,0:T(4,128)} %order.1, f32[4,192,512]{2,1,0:T(8,128)} %bitcast.2, f32[7,4,192,384]{3,2,1,0:T(8,128)} %transfer.1, f32[4,192,512]{2,1,0:T(8,128)} %bitcast.3), custom_call_target="tpu_custom_call" | custom-call | tf_op jit(solution)/shard_map/pallas_call | solution.py:264
  92.9 2.1 %shard_map.56 = f32[2048,512]{1,0:T(8,128)} custom-call(f32[2048,512]{1,0:T(8,128)S(1)} %shard_map.55.result), custom_call_target="tpu_custom_call" | custom-call | tf_op jit(solution)/shard_map/pallas_call | solution.py:292

commit v3 on v2

--- a/solution.py
+++ b/solution.py
@@ -12,7 +12,8 @@
 WIDTH = 128
 MIDDLE = 2
 FAR = 3
-SLOTS = 4
+NEAR = 1
+LAST = 1
 LEAD = 1
 FLIGHT = 8
 VMEM_BYTES = 67043328
@@ -43,7 +44,7 @@
 def kernel(
     stages, offsets, low_bits,
     rhs, order, source, transfer, target, out,
-    order_v, chosen, rhs_v, source_v, target_v, transfer_v, local_t, stage_t, in_v, placed_v,
+    order_v, chosen, rhs_v, source_v, target_v, transfer_v, in_v, placed_v,
     sent, received, load_sem, rhs_sem, transfer_sem, send_sem, recv_sem,
 ):
     leaf_count, leaf_rows = order.shape
@@ -64,7 +65,7 @@
 
     def load_transfer(level):
         return pltpu.make_async_copy(
-            transfer.at[level], transfer_v.at[level % SLOTS], transfer_sem.at[max(level - low_bits + 1, 0)]
+            transfer.at[level], transfer_v.at[level], transfer_sem.at[max(level - low_bits + 1, 0)]
         )
 
     low_slots = transfer_v.at[pl.ds(0, low_bits)]
@@ -86,24 +87,6 @@
             placed_v[leaf, index] = lax.dot_general(
                 chosen[leaf], part, (((1,), (1,)), ((), ())), preferred_element_type=F32
             ).astype(BF16)
-
-    def prepare_local(level):
-        for node in range(leaf_count):
-            for index, part in enumerate(split(transfer_v[level % SLOTS, node])):
-                local_t[level, node, index] = part
-
-    def prepare(stage):
-        level = low_bits + stage
-        load_transfer(level).wait()
-
-        @pl.loop(0, leaf_count)
-        def _(node):
-            for index, part in enumerate(split(transfer_v[level % SLOTS, node])):
-                stage_t[stage, node, index, 0] = part[:, :rank]
-                stage_t[stage, node, index, 1] = part[:, rank:]
-
-        if level + SLOTS < levels:
-            load_transfer(level + SLOTS).start()
 
     def exchange(stage, unit):
         return pltpu.make_async_remote_copy(
@@ -115,11 +98,8 @@
             device_id_type=pl.DeviceIdType.MESH,
         )
 
-    def half(stage, node, side, value):
-        return dot3(stage_t[stage, node, 0, side], stage_t[stage, node, 1, side], value)
-
     def combine(level, node, own, other):
-        return dot3(local_t[level, node, 0], local_t[level, node, 1], jnp.concatenate([own, other], axis=0))
+        return dot3(*split(transfer_v[level, node]), jnp.concatenate([own, other], axis=0))
 
     def enter(chunk, first=False):
         load_rhs(chunk).wait()
@@ -131,8 +111,6 @@
         def value_of(level, node):
             if (level, node) not in current:
                 bit = level - 1
-                if first and all((level, other) not in current for other in range(leaf_count)):
-                    prepare_local(bit)
                 current[level, node] = combine(bit, node, value_of(bit, node), value_of(bit, node ^ 2**bit))
             return current[level, node]
 
@@ -146,7 +124,6 @@
 
     def advance(stage, unit):
         node = unit % leaf_count
-        own = half(stage, node, 0, sent[stage, unit])
         exchange(stage, unit).wait_recv()
         if stage == 0:
 
@@ -154,7 +131,7 @@
             def _():
                 exchange(0, unit + LEAD).start()
 
-        value = own + half(stage, node, 1, received[stage, unit])
+        value = combine(low_bits + stage, node, sent[stage, unit], received[stage, unit])
         if stage + 1 < count:
             sent[stage + 1, unit] = value
             exchange(stage + 1, unit).start()
@@ -166,31 +143,29 @@
 
     load_order.start()
     load_source.start()
-    load_rhs(0).start()
     barrier = pltpu.get_barrier_semaphore()
     for stage in stages:
         pl.semaphore_signal(barrier, inc=1, device_id=partner_id(*stage), device_id_type=pl.DeviceIdType.MESH)
     load_order.wait()
+    load_rhs(0).start()
     for level in range(low_bits):
         load_transfer(level).start()
     for leaf in range(leaf_count):
         select(leaf)
+    load_transfer(low_bits).start()
+    load_rhs(1).start()
     load_source.wait()
     for leaf in range(leaf_count):
         place_in(leaf)
-    for level in range(low_bits, min(SLOTS, levels)):
-        load_transfer(level).start()
-    load_rhs(1).start()
     if low_bits:
         low_transfer.wait()
     enter(0, first=True)
-    for level in range(SLOTS, min(SLOTS + low_bits, levels)):
+    for level in range(low_bits + 1, levels):
         load_transfer(level).start()
     load_target.start()
     for chunk in range(2, chunks):
         load_rhs(chunk).start()
-    prepare(0)
-    prepare(1)
+    enter(1)
 
     near = [stage for stage in range(count) if stages[stage] == ("col", 0)]
     turns = near + [stage for stage in reversed(range(count)) if stage not in near]
@@ -200,15 +175,13 @@
         for stage in turns:
             unit = tick - offsets[stage]
 
+            @pl.when(unit == 0)
+            def _():
+                load_transfer(low_bits + stage).wait()
+
             @pl.when((unit >= 0) & (unit < units))
             def _():
                 advance(stage, unit)
-
-        for stage in range(2, count):
-
-            @pl.when(tick == stage - 2)
-            def _():
-                prepare(stage)
 
         @pl.when((tick >= offsets[-1] - leaf_count) & (tick < offsets[-1]))
         def _():
@@ -220,7 +193,7 @@
 
             place_out(leaf)
 
-        @pl.when((tick % leaf_count == 1) & (tick // leaf_count + 1 < chunks))
+        @pl.when((tick % leaf_count == 1) & (tick > leaf_count) & (tick // leaf_count + 1 < chunks))
         def _():
             enter(tick // leaf_count + 1)
 
@@ -254,7 +227,7 @@
     offsets = [0]
     for axis, bit in stages[1:]:
         if axis == "col":
-            offsets.append(offsets[-1] + 1)
+            offsets.append(offsets[-1] + (NEAR if bit == 0 else LAST))
         else:
             offsets.append(offsets[-1] + (FAR if bit == row_bits - 1 else MIDDLE))
     chunks = columns // WIDTH
@@ -272,9 +245,7 @@
             pltpu.VMEM((chunks, points, WIDTH), F32),
             pltpu.VMEM((leaf_count, rank, leaf_rows), F32),
             pltpu.VMEM((leaf_count, rank, leaf_rows), F32),
-            pltpu.VMEM((SLOTS,) + transfer.shape[1:], F32),
-            pltpu.VMEM((low_bits, leaf_count, 2, rank, 2 * rank), BF16),
-            pltpu.VMEM((count, leaf_count, 2, 2, rank, rank), BF16),
+            pltpu.VMEM(transfer.shape, F32),
             pltpu.VMEM((leaf_count, 2 * rank, leaf_rows), BF16),
             pltpu.VMEM((leaf_count, 2, leaf_rows, rank), BF16),
             pltpu.VMEM((count, units, rank, WIDTH), F32),

time: 95.2 us -> 94.6 us (level)
  no operation moved by 1% of the time
where the time goes in v3:
time: 94.6 us; the launch traced here: 94.4 us
  Pallas kernels  94.4 us (100%)
    pallas_call x1, Pallas kernels, on_device(): pl.pallas_call(functools.partial(kernel, stages, offsets, low_bits), out_...  92.3 us
    pallas_call x1, Pallas kernels, on_device(): pl.pallas_call(output_kernel, out_shape=jax.ShapeDtypeStruct((points, col...  2.07 us

profile of v3, /device:TPU:0, one launch (start us, length us, event | category | flops | bytes accessed | tf_op | source)
XLA Modules:
  0.0 94.4 jit_solution(10486399456714177027)
XLA Ops:
  0.0 92.3 %shard_map.55.result = f32[2048,512]{1,0:T(8,128)S(1)} custom-call(f32[2048,512]{1,0:T(8,128)} %rhs.1, s32[4,512]{1,0:T(4,128)} %order.1, f32[4,192,512]{2,1,0:T(8,128)} %bitcast.2, f32[7,4,192,384]{3,2,1,0:T(8,128)} %transfer.1, f32[4,192,512]{2,1,0:T(8,128)} %bitcast.3), custom_call_target="tpu_custom_call" | custom-call | tf_op jit(solution)/shard_map/pallas_call | solution.py:237
  92.3 2.1 %shard_map.56 = f32[2048,512]{1,0:T(8,128)} custom-call(f32[2048,512]{1,0:T(8,128)S(1)} %shard_map.55.result), custom_call_target="tpu_custom_call" | custom-call | tf_op jit(solution)/shard_map/pallas_call | solution.py:263

commit v4 on v3

--- a/solution.py
+++ b/solution.py
@@ -13,7 +13,7 @@
 MIDDLE = 2
 FAR = 3
 NEAR = 1
-LAST = 1
+LAST = 2
 LEAD = 1
 FLIGHT = 8
 VMEM_BYTES = 67043328
@@ -170,10 +170,12 @@
     near = [stage for stage in range(count) if stages[stage] == ("col", 0)]
     turns = near + [stage for stage in reversed(range(count)) if stage not in near]
 
-    @pl.loop(0, units + offsets[-1])
+    behind = lax.axis_index("col") % 2
+
+    @pl.loop(0, units + offsets[-1] + 1)
     def _(tick):
         for stage in turns:
-            unit = tick - offsets[stage]
+            unit = tick - offsets[stage] - (behind if near and stage >= near[0] else 0)
 
             @pl.when(unit == 0)
             def _():

time: 94.6 us -> 93.4 us (0.987)
  Pallas kernels: 94.4 us -> 93.2 us
    pallas_call x1, Pallas kernels: 92.3 us -> 91.1 us  [on_device(): pl.pallas_call(functools.partial(kernel, stages, offsets, low_bits), out_...]
where the time goes in v4:
time: 93.4 us; the launch traced here: 93.2 us
  Pallas kernels  93.2 us (100%)
    pallas_call x1, Pallas kernels, on_device(): pl.pallas_call(functools.partial(kernel, stages, offsets, low_bits), out_...  91.1 us
    pallas_call x1, Pallas kernels, on_device(): pl.pallas_call(output_kernel, out_shape=jax.ShapeDtypeStruct((points, col...  2.07 us

profile of v4, /device:TPU:0, one launch (start us, length us, event | category | flops | bytes accessed | tf_op | source)
XLA Modules:
  0.0 93.2 jit_solution(9230025970643846218)
XLA Ops:
  0.0 91.1 %shard_map.55.result = f32[2048,512]{1,0:T(8,128)S(1)} custom-call(f32[2048,512]{1,0:T(8,128)} %rhs.1, s32[4,512]{1,0:T(4,128)} %order.1, f32[4,192,512]{2,1,0:T(8,128)} %bitcast.2, f32[7,4,192,384]{3,2,1,0:T(8,128)} %transfer.1, f32[4,192,512]{2,1,0:T(8,128)} %bitcast.3), custom_call_target="tpu_custom_call" | custom-call | tf_op jit(solution)/shard_map/pallas_call | solution.py:239
  91.1 2.1 %shard_map.56 = f32[2048,512]{1,0:T(8,128)} custom-call(f32[2048,512]{1,0:T(8,128)S(1)} %shard_map.55.result), custom_call_target="tpu_custom_call" | custom-call | tf_op jit(solution)/shard_map/pallas_call | solution.py:265

commit v5 on v4

--- a/solution.py
+++ b/solution.py
@@ -15,7 +15,7 @@
 NEAR = 1
 LAST = 2
 LEAD = 1
-FLIGHT = 8
+FLIGHT = 6
 VMEM_BYTES = 67043328
 
 

time: 93.4 us -> 93.3 us (level)
  no operation moved by 1% of the time
where the time goes in v5:
time: 93.3 us; the launch traced here: 93.1 us
  Pallas kernels  93.1 us (100%)
    pallas_call x1, Pallas kernels, on_device(): pl.pallas_call(functools.partial(kernel, stages, offsets, low_bits), out_...  91 us
    pallas_call x1, Pallas kernels, on_device(): pl.pallas_call(output_kernel, out_shape=jax.ShapeDtypeStruct((points, col...  2.07 us

profile of v5, /device:TPU:0, one launch (start us, length us, event | category | flops | bytes accessed | tf_op | source)
XLA Modules:
  0.0 93.1 jit_solution(17670477165945416426)
XLA Ops:
  0.0 91.0 %shard_map.55.result = f32[2048,512]{1,0:T(8,128)S(1)} custom-call(f32[2048,512]{1,0:T(8,128)} %rhs.1, s32[4,512]{1,0:T(4,128)} %order.1, f32[4,192,512]{2,1,0:T(8,128)} %bitcast.2, f32[7,4,192,384]{3,2,1,0:T(8,128)} %transfer.1, f32[4,192,512]{2,1,0:T(8,128)} %bitcast.3), custom_call_target="tpu_custom_call" | custom-call | tf_op jit(solution)/shard_map/pallas_call | solution.py:239
  91.0 2.1 %shard_map.56 = f32[2048,512]{1,0:T(8,128)} custom-call(f32[2048,512]{1,0:T(8,128)S(1)} %shard_map.55.result), custom_call_target="tpu_custom_call" | custom-call | tf_op jit(solution)/shard_map/pallas_call | solution.py:265
